TPU v7x, 256 devices: a whole 4x4x8 slice. The times are simulated.
256 devices in a mesh: pts: 8 (over x, core), rows: 32 (over z, y).
Axes of the slice: x: 4, y: 4, z: 8, core: 2. Of those that a mesh axis runs over, the one named last changes fastest.
Arguments:
- solutions: bfloat16 [16, 262144, 128], P('pts', 'rows'), may hold values from -6 to 6
- probe: bfloat16 [64, 262144], P(None, 'rows'), may hold values from -0.01171875 to 0.01171875
- left_factor: float32 [256, 256], replicated, may hold values from -0.375 to 0.375
- singular: float32 [256], replicated, may hold values from 1 to 13.8, as said below
- right_factor: float32 [256, 256], replicated, may hold values from -0.375 to 0.375
- reduced_adjoint: float32 [256, 256], replicated, may hold values from -6 to 6
Outputs:
- solution_adjoint: bfloat16 [16, 262144, 128], P('pts', 'rows')
Inputs may be any that keep to these rules, and one draw needn't show every extreme that they name: `singular`: rising, each value at least 0.03 above the one before.
All inputs are finite; a program needn't handle non-finite values.
Results may differ from a plain program's by a relative error of at most 0.0049.
Values sent between devices are 32-bit elements; how exact they have to be, the bound alone decides.
A program may use at most 64 MiB of HBM per device.

v0:
```python
import math

import jax
import jax.numpy as jnp
from jax import lax
from jax.sharding import PartitionSpec as P

L = 64
K = 4


def coefficients(first, count, total, orders):
    theta = math.pi * (first + jnp.arange(count, dtype=jnp.float32) + 0.5) / total
    angle = theta[:, None] * orders[None, :]
    return (jnp.cos(angle) / total, jnp.sin(angle) / total)


def matmul(first, second):
    return jnp.dot(
        first, second, precision=lax.Precision.HIGHEST, preferred_element_type=jnp.float32
    )


def svd_back(hankel, left, sing, right, adjoint):
    quot = matmul(left.T, hankel)
    prod_right = matmul(hankel, right)
    zmat = matmul(quot, right)
    zbar = adjoint / sing[None, :]
    sbar = -jnp.sum(adjoint * zmat, axis=0) / (sing * sing)
    ubar = matmul(prod_right, zbar.T)
    wbar = matmul(quot.T, zbar)
    left_term = matmul(left.T, ubar)
    right_term = matmul(right.T, wbar)
    square = sing * sing
    eye_mask = jnp.eye(sing.shape[0], dtype=bool)
    recip = jnp.where(
        eye_mask, 0.0, 1.0 / jnp.where(eye_mask, 1.0, square[None, :] - square[:, None])
    )
    core = (
        recip * (left_term - left_term.T) * sing[None, :]
        + jnp.diag(sbar)
        + sing[:, None] * (recip * (right_term - right_term.T))
    )
    return (core, zbar)


def build_hankel(moments):
    return jnp.concatenate(
        [jnp.concatenate([moments[i + j] for j in range(K)], axis=1) for i in range(K)], axis=0
    )


def per_device(solutions, probe, left_factor, singular, right_factor, reduced_adjoint):
    hi = lax.Precision.HIGHEST
    point_count = solutions.shape[0]
    total = point_count * lax.axis_size("pts")
    first = (lax.axis_index("pts") * point_count).astype(jnp.float32)
    orders = jnp.arange(1, 2 * K + 1, dtype=jnp.float32)
    cos_t, sin_t = coefficients(first, point_count, total, orders)
    gram = jnp.einsum("ln,pnc->plc", probe, solutions, preferred_element_type=jnp.float32)
    moments = lax.psum(
        jnp.einsum("pk,plc->klc", cos_t[:, 1:], gram[:, :, :L], precision=hi)
        - jnp.einsum("pk,plc->klc", sin_t[:, 1:], gram[:, :, L:], precision=hi),
        ("pts", "rows"),
    )
    hankel = build_hankel(moments)
    core, zbar = svd_back(hankel, left_factor, singular, right_factor, reduced_adjoint)
    first_bar = matmul(matmul(left_factor, core), right_factor.T)
    second_bar = matmul(matmul(left_factor, zbar), right_factor.T)
    blocks = [jnp.zeros((L, L), jnp.float32) for k in range(2 * K)]
    for i in range(K):
        for j in range(K):
            blocks[i + j] = blocks[i + j] + first_bar[i * L : (i + 1) * L, j * L : (j + 1) * L]
            blocks[i + j + 1] = (
                blocks[i + j + 1] + second_bar[i * L : (i + 1) * L, j * L : (j + 1) * L]
            )
    moment_adjoint = jnp.stack(blocks)
    weights = jnp.concatenate(
        [
            jnp.einsum("pk,klc->plc", cos_t, moment_adjoint, precision=hi),
            -jnp.einsum("pk,klc->plc", sin_t, moment_adjoint, precision=hi),
        ],
        axis=2,
    ).astype(jnp.bfloat16)
    result = jnp.einsum("ln,plc->pnc", probe, weights, preferred_element_type=jnp.float32)
    return result.astype(jnp.bfloat16)


def solution(mesh):
    in_specs = (P("pts", "rows", None), P(None, "rows"), P(), P(), P(), P())
    out_specs = P("pts", "rows", None)
    return jax.shard_map(
        per_device, mesh=mesh, in_specs=in_specs, out_specs=out_specs, check_vma=False
    )
```

profile of v0, /device:TPU:1, one launch (start us, length us, event | category | flops | bytes accessed | tf_op | source)
XLA Modules:
  0.0 295.4 jit_solution(6354948563807823471)
XLA Ops:
  6.6 1.1 copy-done
  7.8 3.0 %convolution_bitcast_fusion = f32[2,64,128]{2,1,0:T(8,128)S(1)} fusion(bf16[2,8192,128]{2,1,0:T(8,128)(2,1)} %param.6, bf16[64,8192]{1,0:T(8,128)(2,1)S(1)} %copy-done), kind=kOutput, calls=%fused_computation.5 | convolution fusion | flops 268435456 | bytes 5308416 | tf_op jit(solution)/shard_map/ln,pnc->plc/dot_general | solution.py:60
  10.8 0.1 fusion.51
  10.9 0.5 fusion.31
  11.5 1.2 convolution_subtract_fusion
  12.7 0.6 fusion.63
  13.3 0.6 fusion.73
  13.9 255.6 %all-reduce.2.cloned.1.call-done = f32[7,64,64]{2,0,1:T(8,128)} async-done(((f32[7,64,64]{2,0,1:T(8,128)}), f32[7,64,64]{2,0,1:T(8,128)}) %all-reduce.2.cloned.1.call-update) | async-done | bytes 114704 | tf_op jit(solution)/shard_map/psum | solution.py:61
  269.6 2.1 fusion.68
  271.7 0.7 fusion.66
  272.4 0.6 fusion.1
  273.0 0.4 fusion.64
  273.4 0.4 fusion.67
  273.9 0.6 fusion.71
  274.5 0.4 fusion.65
  274.9 0.6 fusion.70
  275.5 0.1 copy.15
  275.6 0.1 copy.16
  275.8 0.7 fusion.7
  276.5 0.6 fusion.72
  277.8 0.5 fusion.20
  278.3 0.5 fusion.18
  278.9 3.3 %fusion = bf16[2,8192,128]{1,2,0:T(8,128)(2,1)} fusion(bf16[64,8192]{1,0:T(8,128)(2,1)S(1)} %copy-done, bf16[2,64,64]{2,1,0:T(8,128)(2,1)S(1)} %fusion.29, bf16[2,64,64]{2,1,0:T(8,128)(2,1)S(1)} %copy.39), kind=kOutput, calls=%fused_computation.1 | convolution fusion | flops 270598144 | bytes 5275648 | tf_op jit(solution)/shard_map/ln,plc->pnc/dot_general | solution.py:85
  282.2 6.3 %copy.17 = bf16[2,8192,128]{2,1,0:T(8,128)(2,1)} copy(bf16[2,8192,128]{1,2,0:T(8,128)(2,1)} %fusion) | data formatting | bytes 8388608 | tf_op jit(solution)/shard_map/convert_element_type | solution.py:86
  (25 shorter events, 0.8 us)
Async XLA Ops:
  6.5 1.2 copy-start
  6.5 6.2 %copy-start.4 = (f32[256]{0:T(256)S(1)}, f32[256]{0:T(256)}, u32[]{:S(2)}) copy-start(f32[256]{0:T(256)} %param.9) | copy-start | bytes 3076
  6.5 6.2 %copy-start.3 = (f32[256,256]{1,0:T(8,128)S(1)}, f32[256,256]{1,0:T(8,128)}, u32[]{:S(2)}) copy-start(f32[256,256]{1,0:T(8,128)} %param.11) | copy-start | bytes 786436
  6.5 6.2 %copy-start.2 = (f32[256,256]{1,0:T(8,128)S(1)}, f32[256,256]{1,0:T(8,128)}, u32[]{:S(2)}) copy-start(f32[256,256]{1,0:T(8,128)} %param.8) | copy-start | bytes 786436
  6.5 6.8 %copy-start.1 = (f32[256,256]{1,0:T(8,128)S(1)}, f32[256,256]{1,0:T(8,128)}, u32[]{:S(2)}) copy-start(f32[256,256]{1,0:T(8,128)} %param.10) | copy-start | bytes 786436
  6.5 263.0 %all-reduce.2.cloned.1.call-start = ((), (), s32[]{:S(2)}) async-start(), calls=%async_computation | async-start | bytes 524288 | tf_op jit(solution)/shard_map/psum | solution.py:61
Sparse Core Ops, SparseCore 0:
  12.8 256.6 all-reduce.1
where the time goes:
time: 296 us; the launch traced here: 295 us
  waiting for transfers between devices  256 us (86%)
  matrix products  15.4 us (5%)
  between operations  13.7 us (5%)
  local copies, waits for them, and re-layouts  9.97 us (3%)
    psum x1, waiting for transfers between devices, per_device(): lax.psum(jnp.einsum('pk,plc->klc', cos_t[:, 1:], gram[:, :, :L], precisio...  256 us
    dot_general x11, matrix products, matmul(): jnp.dot(first, second, precision=lax.Precision.HIGHEST, preferred_element...  6.33 us
    convert_element_type x1, local copies, waits for them, and re-layouts, per_device(): return result.astype(jnp.bfloat16)  6.31 us
  transfers between devices with their start and end apart: 1, of which 1 were waited for; matrix products, arithmetic and copies ran while one was open for 0% of the time, Pallas kernels for 0%

commit v1 on v0

v1 whole, which is shorter than its diff:
```python
import functools
import math

import jax
import jax.numpy as jnp
import numpy as np
from jax import lax
from jax.experimental import pallas as pl
from jax.experimental.pallas import tpu as pltpu
from jax.sharding import PartitionSpec as P

L = 64
K = 4
HANK = 256
PTS = 16
MESH = pl.DeviceIdType.MESH
X, Y, Z, CORES = 4, 4, 8, 2
PIECE = 8
GROUP = X * Y * CORES
CHUNKS = 8


def coefficient_table():
    theta = math.pi * (np.arange(PTS) + 0.5) / PTS
    cos = lambda m: np.cos(m * theta)[:, None] * np.ones((1, L)) / PTS
    sin = lambda m: np.sin(m * theta)[:, None] * np.ones((1, L)) / PTS
    table = np.zeros((PTS, 16, 2 * L))
    for q in range(4):
        table[:, q, :L] = cos(2 * q + 2)
        table[:, 4 + q, :L] = -sin(2 * q + 2)
        if q < 3:
            table[:, q, L:] = -sin(2 * q + 3)
            table[:, 4 + q, L:] = cos(2 * q + 3)
    for k in range(2 * K):
        table[:, 8 + k, :L] = cos(k + 1)
        table[:, 8 + k, L:] = -sin(k + 1)
    return table.astype(np.float32)


def split(value):
    high = value.astype(jnp.bfloat16)
    low = (value - high.astype(jnp.float32)).astype(jnp.bfloat16)
    return high, low


def lhs3(value):
    high, low = split(value)
    return jnp.concatenate([high, high, low], axis=1)


def rhs3(value):
    high, low = split(value)
    return jnp.concatenate([high, low, high], axis=0)


def dot(first, second):
    return jnp.dot(first, second, preferred_element_type=jnp.float32)


def diagonal_sums(full):
    tile = lambda i, h: full[L * i : L * (i + 1), 2 * L * h : 2 * L * (h + 1)]
    return [
        tile(0, 0),
        tile(1, 0),
        tile(2, 0) + tile(0, 1),
        tile(3, 0) + tile(1, 1),
        tile(2, 1),
        tile(3, 1),
    ]


def reduce_kernel(
    sol, probe, left, sing, right, adj, table, w_out,
    solv, probev, leftv, rightv, adjv, singv, tabv,
    send_a, recv_a, recv_b, recv_c,
    lhs_ut, rhs_w, rhs_zt, lhs_zt, lhs_u, rhs_wt, f_row, f_col, second,
    chunk_sem, small_sem, send_sem, recv_sem,
):
    pts = lax.axis_index("pts")
    rows = lax.axis_index("rows")
    x, core = pts // CORES, pts % CORES
    z, y = rows // Y, rows % Y
    me = y * (X * CORES) + pts
    depth = sol.shape[1]
    size = depth // CHUNKS

    plane = []
    for dx, dy in sorted(
        [(i, j) for i in range(X) for j in range(Y)],
        key=lambda d: -(min(d[0], X - d[0]) + min(d[1], Y - d[1])),
    ):
        for dc in range(CORES):
            if dx or dy or dc:
                other = ((x + dx) % X) * CORES + (core + dc) % CORES
                other_y = (y + dy) % Y
                plane.append((other, z * Y + other_y, other_y * (X * CORES) + other))
    line = []
    for dz in sorted(range(1, Z), key=lambda d: -min(d, Z - d)):
        line.append((pts, ((z + dz) % Z) * Y + y))

    copies = []
    for c in range(CHUNKS):
        part = pl.ds(c * size, size)
        group = [pltpu.make_async_copy(probe.at[:, part], probev.at[:, part], chunk_sem.at[c, 0])]
        for p in range(2):
            group.append(
                pltpu.make_async_copy(
                    sol.at[p, part, :], solv.at[part, pl.ds(128 * p, 128)], chunk_sem.at[c, 1 + p]
                )
            )
        for copy in group:
            copy.start()
        copies.append(group)
    small = [
        pltpu.make_async_copy(table.at[pl.ds(pts * 2, 2)], tabv, small_sem.at[0]),
        pltpu.make_async_copy(sing, singv, small_sem.at[1]),
        pltpu.make_async_copy(left, leftv, small_sem.at[2]),
        pltpu.make_async_copy(right, rightv, small_sem.at[3]),
        pltpu.make_async_copy(adj, adjv, small_sem.at[4]),
    ]
    for copy in small:
        copy.start()

    barrier = pltpu.get_barrier_semaphore()
    for p, r in line + [(p, r) for p, r, _ in plane]:
        pl.semaphore_signal(barrier, inc=1, device_id=(p, r), device_id_type=MESH)

    gram = jnp.zeros((L, 256), jnp.float32)
    for c in range(CHUNKS):
        for copy in copies[c]:
            copy.wait()
        part = pl.ds(c * size, size)
        gram = gram + dot(probev[:, part], solv[part, :])
    small[0].wait()
    for q in range(4):
        total = None
        for p in range(2):
            own = gram[:, 128 * p : 128 * (p + 1)]
            term = own * tabv[p, q : q + 1, :] + pltpu.roll(own, L, 1) * tabv[p, 4 + q : 5 + q, :]
            total = term if total is None else total + term
        send_a[L * q : L * (q + 1), :] = total

    pl.semaphore_wait(barrier, len(plane) + len(line))
    mine = pl.ds(pl.multiple_of(me * PIECE, PIECE), PIECE)
    for p, r, there in plane:
        pltpu.make_async_remote_copy(
            src_ref=send_a.at[pl.ds(pl.multiple_of(there * PIECE, PIECE), PIECE)],
            dst_ref=recv_a.at[mine],
            send_sem=send_sem.at[0],
            recv_sem=recv_sem.at[0],
            device_id=(p, r),
            device_id_type=MESH,
        ).start()
    recv_a[mine, :] = send_a[mine, :]

    for copy in small[1:]:
        copy.wait()
    s_row = jnp.broadcast_to(singv[...], (HANK, HANK))
    s_col = s_row.T
    zbar = adjv[...] / s_row
    u = leftv[...]
    w = rightv[...]
    lhs_ut[...] = lhs3(u.T)
    rhs_w[...] = rhs3(w)
    lhs_u[...] = lhs3(u)

    many = pl.ds(0, (GROUP - 1) * PIECE)
    everything = lambda ref, n, i: pltpu.make_async_copy(
        ref.at[pl.ds(0, n * PIECE)], ref.at[pl.ds(0, n * PIECE)], i
    )
    everything(recv_a, GROUP - 1, recv_sem.at[0]).wait()
    here = pl.ds(pl.multiple_of(z * PIECE, PIECE), PIECE)
    recv_b[here, :] = jnp.sum(recv_a[...].reshape(GROUP, PIECE, 128), axis=0)
    for p, r in line:
        pltpu.make_async_remote_copy(
            src_ref=recv_b.at[here],
            dst_ref=recv_b.at[here],
            send_sem=send_sem.at[1],
            recv_sem=recv_sem.at[1],
            device_id=(p, r),
            device_id_type=MESH,
        ).start()

    zt = zbar.T
    lhs_zt[...] = lhs3(zt)
    rhs_zt[...] = rhs3(zt)
    rhs_wt[...] = rhs3(w.T)

    everything(recv_b, Z - 1, recv_sem.at[1]).wait()
    recv_c[mine, :] = jnp.sum(recv_b[...].reshape(Z, PIECE, 128), axis=0)
    for p, r, _ in plane:
        pltpu.make_async_remote_copy(
            src_ref=recv_c.at[mine],
            dst_ref=recv_c.at[mine],
            send_sem=send_sem.at[2],
            recv_sem=recv_sem.at[2],
            device_id=(p, r),
            device_id_type=MESH,
        ).start()

    row_id = lax.broadcasted_iota(jnp.int32, (HANK, HANK), 0)
    col_id = lax.broadcasted_iota(jnp.int32, (HANK, HANK), 1)
    eye = row_id == col_id
    recip = jnp.where(eye, 0.0, 1.0 / jnp.where(eye, 1.0, s_row * s_row - s_col * s_col))
    f_row[...] = recip * s_row
    f_col[...] = recip * s_col
    second_bar = dot(lhs3(dot(lhs_u[...], rhs3(zbar))), rhs_wt[...])
    for m, value in enumerate(diagonal_sums(second_bar)):
        second[m] = value

    everything(recv_c, GROUP - 1, recv_sem.at[2]).wait()
    lane = lax.broadcasted_iota(jnp.int32, (L, 2 * L), 1)
    low = lane < L
    even = [recv_c[L * q : L * (q + 1), :] for q in range(4)]
    turned = [pltpu.roll(value, L, 1) for value in even]
    pairs = []
    for q in range(3):
        pairs.append(even[q])
        pairs.append(jnp.where(low, turned[q], turned[q + 1]))
    hankel = jnp.concatenate(
        [jnp.concatenate([pairs[i], pairs[i + 2]], axis=1) for i in range(K)], axis=0
    )
    quot = dot(lhs_ut[...], rhs3(hankel))
    zmat = dot(lhs3(quot), rhs_w[...])
    sing_row = singv[...]
    sbar = -jnp.sum(adjv[...] * zmat, axis=0, keepdims=True) / (sing_row * sing_row)
    left_term = dot(lhs3(zmat), rhs_zt[...])
    right_term = dot(lhs_zt[...], rhs3(zmat))
    core_mat = (
        f_row[...] * (left_term - left_term.T)
        - f_col[...] * (right_term - right_term.T)
        + jnp.where(eye, jnp.broadcast_to(sbar, (HANK, HANK)), 0.0)
    )
    first_bar = dot(lhs3(dot(lhs_u[...], rhs3(core_mat))), rhs_wt[...])

    sums = diagonal_sums(first_bar)
    sums = [sums[0]] + [sums[m] + second[m - 1] for m in range(1, 6)] + [second[5]]
    weights = [jnp.zeros((L, 2 * L), jnp.float32) for p in range(2)]
    zero = jnp.zeros((L, 2 * L), jnp.float32)
    for k in range(2 * K):
        here_k = sums[k] if k < 7 else zero
        before = sums[k - 1] if k > 0 else zero
        mixed = jnp.where(low, here_k, before)
        both = mixed + pltpu.roll(mixed, L, 1)
        for p in range(2):
            weights[p] = weights[p] + both * tabv[p, 8 + k : 9 + k, :]
    for p in range(2):
        w_out[:, 128 * p : 128 * (p + 1)] = weights[p].astype(jnp.bfloat16)

    everything(recv_a, GROUP - 1, send_sem.at[0]).wait()
    everything(recv_b, Z - 1, send_sem.at[1]).wait()
    everything(recv_c, GROUP - 1, send_sem.at[2]).wait()


def output_kernel(probe_ref, w_ref, out_ref):
    res = lax.dot_general(
        probe_ref[...], w_ref[...], (((0,), (0,)), ((), ())), preferred_element_type=jnp.float32
    )
    for p in range(2):
        out_ref[p] = res[:, 128 * p : 128 * (p + 1)].astype(jnp.bfloat16)


def per_device(solutions, probe, left_factor, singular, right_factor, reduced_adjoint):
    table = jnp.asarray(coefficient_table())
    depth = solutions.shape[1]
    hbm = pl.BlockSpec(memory_space=pl.ANY)
    f32 = lambda *shape: pltpu.VMEM(shape, jnp.float32)
    bf16 = lambda *shape: pltpu.VMEM(shape, jnp.bfloat16)
    weights = pl.pallas_call(
        reduce_kernel,
        name="moments",
        out_shape=jax.ShapeDtypeStruct((L, 256), jnp.bfloat16),
        in_specs=[hbm] * 7,
        out_specs=pl.BlockSpec(memory_space=pltpu.VMEM),
        scratch_shapes=[
            bf16(depth, 256), bf16(L, depth), f32(HANK, HANK), f32(HANK, HANK), f32(HANK, HANK),
            f32(1, HANK), f32(2, 16, 128),
            f32(GROUP * PIECE, 128), f32(GROUP * PIECE, 128), f32(Z * PIECE, 128), f32(GROUP * PIECE, 128),
            bf16(HANK, 3 * HANK), bf16(3 * HANK, HANK), bf16(3 * HANK, HANK), bf16(HANK, 3 * HANK),
            bf16(HANK, 3 * HANK), bf16(3 * HANK, HANK), f32(HANK, HANK), f32(HANK, HANK), f32(6, L, 2 * L),
            pltpu.SemaphoreType.DMA((CHUNKS, 3)), pltpu.SemaphoreType.DMA((5,)),
            pltpu.SemaphoreType.DMA((3,)), pltpu.SemaphoreType.DMA((3,)),
        ],
        compiler_params=pltpu.CompilerParams(collective_id=0, has_side_effects=True),
    )(solutions, probe, left_factor, singular.reshape(1, HANK), right_factor, reduced_adjoint, table)
    tile = 1024
    return pl.pallas_call(
        output_kernel,
        name="output",
        grid=(depth // tile,),
        out_shape=jax.ShapeDtypeStruct((2, depth, 128), jnp.bfloat16),
        in_specs=[
            pl.BlockSpec((L, tile), lambda i: (0, i)),
            pl.BlockSpec((L, 256), lambda i: (0, 0)),
        ],
        out_specs=pl.BlockSpec((2, tile, 128), lambda i: (0, i, 0)),
    )(probe, weights)


def solution(mesh):
    in_specs = (P("pts", "rows", None), P(None, "rows"), P(), P(), P(), P())
    out_specs = P("pts", "rows", None)
    return jax.shard_map(
        per_device, mesh=mesh, in_specs=in_specs, out_specs=out_specs, check_vma=False
    )
```

time: 296 us -> 35.7 us (0.12)
  waiting for transfers between devices: 256 us -> 0 us
  Pallas kernels: 0 us -> 35.5 us
  matrix products: 15.4 us -> 0 us
  between operations: 13.7 us -> 0.01 us
  local copies, waits for them, and re-layouts: 9.97 us -> 0 us
    psum x1 -> x0, waiting for transfers between devices: 256 us -> none  [per_device(): lax.psum(jnp.einsum('pk,plc->klc', cos_t[:, 1:], gram[:, :, :L], precisio...]
    pallas_call x0 -> x2, Pallas kernels: none -> 35.5 us  [the longest x1 28.5 us: per_device(): pl.pallas_call(reduce_kernel, name='moments', out_shape=jax.ShapeDtypeStr...]
    dot_general x17 -> x0, matrix products: 15.4 us -> none  [the longest x11 6.33 us: matmul(): jnp.dot(first, second, precision=lax.Precision.HIGHEST, preferred_element...]
    convert_element_type x1 -> x0, local copies, waits for them, and re-layouts: 6.31 us -> none  [per_device(): return result.astype(jnp.bfloat16)]
  transfers between devices with their start and end apart: 1 -> 0, of which waited for: 1 -> 0; matrix products, arithmetic and copies ran while one was open for 0% -> 0% of each run, Pallas kernels for 0% -> 0%
where the time goes in v1:
time: 35.7 us; the launch traced here: 35.5 us
  Pallas kernels  35.5 us (99%)
    pallas_call x1, Pallas kernels, per_device(): pl.pallas_call(reduce_kernel, name='moments', out_shape=jax.ShapeDtypeStr...  28.5 us
    pallas_call x1, Pallas kernels, per_device(): pl.pallas_call(output_kernel, name='output', grid=(depth // tile,), out_s...  6.96 us

profile of v1, /device:TPU:1, one launch (start us, length us, event | category | flops | bytes accessed | tf_op | source)
XLA Modules:
  0.0 35.5 jit_solution(13625266074778852403)
XLA Ops:
  0.0 28.5 %moments.1.w_ref = bf16[64,256]{1,0:T(8,128)(2,1)} custom-call(bf16[2,8192,128]{2,1,0:T(8,128)(2,1)} %sol.1, bf16[64,8192]{1,0:T(8,128)(2,1)} %probe_ref.1, f32[256,256]{1,0:T(8,128)} %left.1, f32[1,256]{1,0:T(1,128)} %bitcast.1, f32[256,256]{1,0:T(8,128)} %right.1, f32[256,256]{1,0:T(8,128)} %adj.1, f32[16,16,128]{2,1,0:T(8,128)} %constant.2.clone.table), custom_call_target="tpu_custom_call" | custom-call | tf_op jit(solution)/shard_map/moments/pallas_call | solution.py:269
  28.5 7.0 %output.1 = bf16[2,8192,128]{2,1,0:T(8,128)(2,1)} custom-call(bf16[64,8192]{1,0:T(8,128)(2,1)} %probe_ref.1, bf16[64,256]{1,0:T(8,128)(2,1)} %moments.1.w_ref), custom_call_target="tpu_custom_call" | custom-call | tf_op jit(solution)/shard_map/output/pallas_call | solution.py:287

commit v2 on v1

--- a/solution.py
+++ b/solution.py
@@ -70,7 +70,7 @@
 
 
 def reduce_kernel(
-    sol, probe, left, sing, right, adj, table, w_out,
+    sol, probe, left, sing, right, adj, table, w_out, turned_out,
     solv, probev, leftv, rightv, adjv, singv, tabv,
     send_a, recv_a, recv_b, recv_c,
     lhs_ut, rhs_w, rhs_zt, lhs_zt, lhs_u, rhs_wt, f_row, f_col, second,
@@ -97,6 +97,14 @@
     line = []
     for dz in sorted(range(1, Z), key=lambda d: -min(d, Z - d)):
         line.append((pts, ((z + dz) % Z) * Y + y))
+
+    half = depth // 2
+    step = half // 8
+
+    def turn(first, last):
+        for t in range(first, last):
+            pair = [probev[:, h * half + t * step : h * half + (t + 1) * step] for h in range(2)]
+            turned_out[t * step : (t + 1) * step, :] = jnp.concatenate(pair, axis=0).T
 
     copies = []
     for c in range(CHUNKS):
@@ -163,6 +171,7 @@
     lhs_ut[...] = lhs3(u.T)
     rhs_w[...] = rhs3(w)
     lhs_u[...] = lhs3(u)
+    turn(0, 3)
 
     many = pl.ds(0, (GROUP - 1) * PIECE)
     everything = lambda ref, n, i: pltpu.make_async_copy(
@@ -185,6 +194,7 @@
     lhs_zt[...] = lhs3(zt)
     rhs_zt[...] = rhs3(zt)
     rhs_wt[...] = rhs3(w.T)
+    turn(3, 5)
 
     everything(recv_b, Z - 1, recv_sem.at[1]).wait()
     recv_c[mine, :] = jnp.sum(recv_b[...].reshape(Z, PIECE, 128), axis=0)
@@ -207,6 +217,7 @@
     second_bar = dot(lhs3(dot(lhs_u[...], rhs3(zbar))), rhs_wt[...])
     for m, value in enumerate(diagonal_sums(second_bar)):
         second[m] = value
+    turn(5, 8)
 
     everything(recv_c, GROUP - 1, recv_sem.at[2]).wait()
     lane = lax.broadcasted_iota(jnp.int32, (L, 2 * L), 1)
@@ -252,26 +263,42 @@
     everything(recv_c, GROUP - 1, send_sem.at[2]).wait()
 
 
-def output_kernel(probe_ref, w_ref, out_ref):
-    res = lax.dot_general(
-        probe_ref[...], w_ref[...], (((0,), (0,)), ((), ())), preferred_element_type=jnp.float32
-    )
-    for p in range(2):
-        out_ref[p] = res[:, 128 * p : 128 * (p + 1)].astype(jnp.bfloat16)
+def output_kernel(turned, w_ref, out, held, sem):
+    half = turned.shape[0]
+    size = half // CHUNKS
+    zero = jnp.zeros((L, 256), jnp.bfloat16)
+    wide = [jnp.concatenate([w_ref[...], zero], axis=0), jnp.concatenate([zero, w_ref[...]], axis=0)]
+    copies = []
+    for c in range(CHUNKS):
+        block = turned[c * size : (c + 1) * size, :]
+        for h in range(2):
+            res = dot(block, wide[h]).astype(jnp.bfloat16)
+            part = pl.ds(h * half + c * size, size)
+            for p in range(2):
+                held[p, part, :] = res[:, 128 * p : 128 * (p + 1)]
+                copy = pltpu.make_async_copy(held.at[p, part, :], out.at[p, part, :], sem.at[c, h, p])
+                copy.start()
+                copies.append(copy)
+    for copy in copies:
+        copy.wait()
 
 
 def per_device(solutions, probe, left_factor, singular, right_factor, reduced_adjoint):
     table = jnp.asarray(coefficient_table())
     depth = solutions.shape[1]
-    hbm = pl.BlockSpec(memory_space=pl.ANY)
+    hbm = pl.BlockSpec(memory_space=pltpu.HBM)
+    vmem = pl.BlockSpec(memory_space=pltpu.VMEM)
     f32 = lambda *shape: pltpu.VMEM(shape, jnp.float32)
     bf16 = lambda *shape: pltpu.VMEM(shape, jnp.bfloat16)
-    weights = pl.pallas_call(
+    weights, turned = pl.pallas_call(
         reduce_kernel,
         name="moments",
-        out_shape=jax.ShapeDtypeStruct((L, 256), jnp.bfloat16),
+        out_shape=[
+            jax.ShapeDtypeStruct((L, 256), jnp.bfloat16),
+            jax.ShapeDtypeStruct((depth // 2, 128), jnp.bfloat16),
+        ],
         in_specs=[hbm] * 7,
-        out_specs=pl.BlockSpec(memory_space=pltpu.VMEM),
+        out_specs=[vmem] * 2,
         scratch_shapes=[
             bf16(depth, 256), bf16(L, depth), f32(HANK, HANK), f32(HANK, HANK), f32(HANK, HANK),
             f32(1, HANK), f32(2, 16, 128),
@@ -281,20 +308,26 @@
             pltpu.SemaphoreType.DMA((CHUNKS, 3)), pltpu.SemaphoreType.DMA((5,)),
             pltpu.SemaphoreType.DMA((3,)), pltpu.SemaphoreType.DMA((3,)),
         ],
-        compiler_params=pltpu.CompilerParams(collective_id=0, has_side_effects=True),
-    )(solutions, probe, left_factor, singular.reshape(1, HANK), right_factor, reduced_adjoint, table)
-    tile = 1024
+        compiler_params=pltpu.CompilerParams(
+            collective_id=0, has_side_effects=True, vmem_limit_bytes=24 << 20
+        ),
+    )(
+        *(
+            pltpu.with_memory_space_constraint(array, pltpu.HBM)
+            for array in (
+                solutions, probe, left_factor, singular.reshape(1, HANK), right_factor, reduced_adjoint, table
+            )
+        )
+    )
     return pl.pallas_call(
         output_kernel,
         name="output",
-        grid=(depth // tile,),
         out_shape=jax.ShapeDtypeStruct((2, depth, 128), jnp.bfloat16),
-        in_specs=[
-            pl.BlockSpec((L, tile), lambda i: (0, i)),
-            pl.BlockSpec((L, 256), lambda i: (0, 0)),
-        ],
-        out_specs=pl.BlockSpec((2, tile, 128), lambda i: (0, i, 0)),
-    )(probe, weights)
+        in_specs=[vmem] * 2,
+        out_specs=pl.BlockSpec(memory_space=pltpu.HBM),
+        scratch_shapes=[bf16(2, depth, 128), pltpu.SemaphoreType.DMA((CHUNKS, 2, 2))],
+        compiler_params=pltpu.CompilerParams(vmem_limit_bytes=24 << 20),
+    )(turned, weights)
 
 
 def solution(mesh):

time: 35.7 us -> 30.4 us (0.85)
  Pallas kernels: 35.5 us -> 30.3 us
    pallas_call x2, Pallas kernels: 35.5 us -> 30.3 us  [the longest x1 27.8 us: per_device(): pl.pallas_call(reduce_kernel, name='moments', out_shape=[jax.ShapeDtypeSt...]
where the time goes in v2:
time: 30.4 us; the launch traced here: 30.3 us
  Pallas kernels  30.3 us (100%)
    pallas_call x1, Pallas kernels, per_device(): pl.pallas_call(reduce_kernel, name='moments', out_shape=[jax.ShapeDtypeSt...  27.8 us
    pallas_call x1, Pallas kernels, per_device(): pl.pallas_call(output_kernel, name='output', out_shape=jax.ShapeDtypeStru...  2.54 us

profile of v2, /device:TPU:1, one launch (start us, length us, event | category | flops | bytes accessed | tf_op | source)
XLA Modules:
  0.0 30.3 jit_solution(4435702927892160165)
XLA Ops:
  0.0 27.8 %moments.1 = (bf16[64,256]{1,0:T(8,128)(2,1)S(1)}, bf16[4096,128]{1,0:T(8,128)(2,1)S(1)}) custom-call(bf16[2,8192,128]{2,1,0:T(8,128)(2,1)} %sol.1, bf16[64,8192]{1,0:T(8,128)(2,1)} %probe.1, f32[256,256]{1,0:T(8,128)} %left.1, f32[1,256]{1,0:T(1,128)} %bitcast.1, f32[256,256]{1,0:T(8,128)} %right.1, f32[256,256]{1,0:T(8,128)} %adj.1, ...), custom_call_target="tpu_custom_call" | custom-call | tf_op jit(solution)/shard_map/moments/pallas_call | solution.py:293
  27.8 2.5 %output.1 = bf16[2,8192,128]{2,1,0:T(8,128)(2,1)} custom-call(bf16[4096,128]{1,0:T(8,128)(2,1)S(1)} %get-tuple-element.7.turned, bf16[64,256]{1,0:T(8,128)(2,1)S(1)} %get-tuple-element.8.w_ref), custom_call_target="tpu_custom_call" | custom-call | tf_op jit(solution)/shard_map/output/pallas_call | solution.py:322

commit v3 on v2

v3 whole, which is shorter than its diff:
```python
import functools
import math

import jax
import jax.numpy as jnp
import numpy as np
from jax import lax
from jax.experimental import pallas as pl
from jax.experimental.pallas import tpu as pltpu
from jax.sharding import PartitionSpec as P

L = 64
K = 4
HANK = 256
PTS = 16
MESH = pl.DeviceIdType.MESH
X, Y, Z, CORES = 4, 4, 8, 2
PIECE = 8
GROUP = X * Y * CORES
CHUNKS = 8
OUT_ROWS = 128


def coefficient_table():
    theta = math.pi * (np.arange(PTS) + 0.5) / PTS
    cos = lambda m: np.cos(m * theta)[:, None] * np.ones((1, L)) / PTS
    sin = lambda m: np.sin(m * theta)[:, None] * np.ones((1, L)) / PTS
    table = np.zeros((PTS, 16, 2 * L))
    for q in range(4):
        table[:, q, :L] = cos(2 * q + 2)
        table[:, 4 + q, :L] = -sin(2 * q + 2)
        if q < 3:
            table[:, q, L:] = -sin(2 * q + 3)
            table[:, 4 + q, L:] = cos(2 * q + 3)
    for k in range(2 * K):
        table[:, 8 + k, :L] = cos(k + 1)
        table[:, 8 + k, L:] = -sin(k + 1)
    return table.astype(np.float32)


def split(value):
    high = value.astype(jnp.bfloat16)
    low = (value - high.astype(jnp.float32)).astype(jnp.bfloat16)
    return high, low


def dot(first, second):
    return jnp.dot(first, second, preferred_element_type=jnp.float32)


def product(accs, first, second):
    quarter = HANK // 4
    for unit in range(2):
        pltpu.matmul_push_rhs(second[0], 0, unit)
        pltpu.matmul_push_rhs(second[1], 1, unit)
    for unit in range(2):
        for b in range(2):
            part = slice((2 * unit + b) * quarter, (2 * unit + b + 1) * quarter)
            pltpu.matmul_acc_lhs(accs[2 * unit + b], first[0][part], 0 if b == 0 else None)
            pltpu.matmul_acc_lhs(accs[2 * unit + b], first[1][part])
    for unit in range(2):
        for b in range(2):
            part = slice((2 * unit + b) * quarter, (2 * unit + b + 1) * quarter)
            pltpu.matmul_acc_lhs(accs[2 * unit + b], first[0][part], 1 if b == 0 else None)
    return jnp.concatenate([pltpu.matmul_pop(acc) for acc in accs], axis=0)


def diagonal_sums(full):
    tile = lambda i, h: full[L * i : L * (i + 1), 2 * L * h : 2 * L * (h + 1)]
    return [
        tile(0, 0),
        tile(1, 0),
        tile(2, 0) + tile(0, 1),
        tile(3, 0) + tile(1, 1),
        tile(2, 1),
        tile(3, 1),
    ]


def reduce_body(
    sol, probe, left, sing, right, adj, table, w_out, turned_out,
    solv, probev, factors, singv, tabv, send_a, recv_a, recv_b, recv_c,
    ut_ref, w_ref, zt_ref, u_ref, wt_ref, f_row, f_col, second,
    chunk_sem, small_sem, send_sem, recv_sem, *accs
):
    pts = lax.axis_index("pts")
    rows = lax.axis_index("rows")
    x, core = lax.div(pts, CORES), lax.rem(pts, CORES)
    z, y = lax.div(rows, Y), lax.rem(rows, Y)
    me = y * (X * CORES) + pts
    depth = sol.shape[1]
    size = depth // CHUNKS
    half = depth // 2

    copies = []
    for c in range(CHUNKS):
        if c % (CHUNKS // 2) == 0:
            part = pl.ds((2 * c // CHUNKS) * half, half)
            copy = pltpu.make_async_copy(probe.at[:, part], probev.at[:, part], chunk_sem.at[CHUNKS + 2 * c // CHUNKS])
            copy.start()
            copies.append(copy)
        part = pl.ds(c * size, size)
        copy = pltpu.make_async_copy(sol.at[:, part], solv.at[:, part], chunk_sem.at[c])
        copy.start()
        copies.append(copy)
    tab = pltpu.make_async_copy(table.at[pl.ds(pts * 2, 2)], tabv, small_sem.at[0])
    tab.start()

    xs = [lax.rem(x + d, X) * CORES for d in range(X)]
    cores = [core, 1 - core]
    ys = [lax.rem(y + d, Y) for d in range(Y)]
    zs = [lax.rem(z + d, Z) * Y + y for d in range(Z)]
    plane = []
    for dx, dy in sorted(
        [(i, j) for i in range(X) for j in range(Y)],
        key=lambda d: -(min(d[0], X - d[0]) + min(d[1], Y - d[1])),
    ):
        for dc in range(CORES):
            if dx or dy or dc:
                other = xs[dx] + cores[dc]
                plane.append((other, z * Y + ys[dy], ys[dy] * (X * CORES) + other))
    line = [(pts, zs[d]) for d in sorted(range(1, Z), key=lambda d: -min(d, Z - d))]

    barrier = pltpu.get_barrier_semaphore()
    for p, r in line[:1] + [(p, r) for p, r, _ in plane] + line[1:]:
        pl.semaphore_signal(barrier, inc=1, device_id=(p, r), device_id_type=MESH)
    small = [pltpu.make_async_copy(sing, singv, small_sem.at[1])]
    small += [pltpu.make_async_copy(ref, factors.at[i], small_sem.at[2]) for i, ref in enumerate((left, right, adj))]
    for copy in small:
        copy.start()

    tile = 0
    done = iter(copies)
    for c in range(CHUNKS):
        if c % (CHUNKS // 2) == 0:
            next(done).wait()
        next(done).wait()
        for start in range(c * size, (c + 1) * size, HANK):
            part = pl.ds(start, HANK)
            unit, register = tile % 2, tile // 2 % 2
            pltpu.matmul_push_rhs(jnp.concatenate([solv[0, part, :], solv[1, part, :]], axis=1), register, unit)
            pltpu.matmul_acc_lhs(accs[2 * unit], probev[:, part], register)
            tile += 1
    gram = pltpu.matmul_pop(accs[0]) + pltpu.matmul_pop(accs[2])
    tab.wait()
    for q in range(4):
        total = None
        for p in range(2):
            own = gram[:, 128 * p : 128 * (p + 1)]
            term = own * tabv[p, q : q + 1, :] + pltpu.roll(own, L, 1) * tabv[p, 4 + q : 5 + q, :]
            total = term if total is None else total + term
        send_a[L * q : L * (q + 1), :] = total

    def piece(index):
        return pl.ds(pl.multiple_of(index * PIECE, PIECE), PIECE)

    def send(peers, source, target, phase):
        @pl.when(rows >= 0)
        def _():
            for peer in peers:
                pltpu.make_async_remote_copy(
                    src_ref=source(peer),
                    dst_ref=target,
                    send_sem=send_sem.at[0],
                    recv_sem=recv_sem.at[phase],
                    device_id=peer[:2],
                    device_id_type=MESH,
                ).start()

    def arrived(ref, count, phase):
        ref = ref.at[pl.ds(0, count * PIECE)]
        pltpu.make_async_copy(ref, ref, recv_sem.at[phase]).wait()

    mine, here = piece(me), piece(z)
    pl.semaphore_wait(barrier, len(plane) + len(line))
    send(plane, lambda peer: send_a.at[piece(peer[2])], recv_a.at[mine], 0)

    def keep(ref, value):
        ref[0], ref[1] = split(value)

    def turn(first, last):
        step = half // 8
        for t in range(first, last):
            pair = [probev[:, h * half + t * step : h * half + (t + 1) * step] for h in range(2)]
            turned_out[t * step : (t + 1) * step, :] = jnp.concatenate(pair, axis=0).T

    recv_a[mine, :] = send_a[mine, :]
    small[0].wait()
    pltpu.make_async_copy(factors, factors, small_sem.at[2]).wait()
    s_row = jnp.broadcast_to(singv[...], (HANK, HANK))
    zbar = factors[2] / s_row
    keep(ut_ref, factors[0].T)
    keep(u_ref, factors[0])
    keep(w_ref, factors[1])
    keep(wt_ref, factors[1].T)
    keep(zt_ref, zbar.T)
    turn(0, 4)

    arrived(recv_a, GROUP - 1, 0)
    recv_b[here, :] = jnp.sum(recv_a[...].reshape(GROUP, PIECE, 128), axis=0)
    send(line, lambda peer: recv_b.at[here], recv_b.at[here], 1)

    row_id = lax.broadcasted_iota(jnp.int32, (HANK, HANK), 0)
    col_id = lax.broadcasted_iota(jnp.int32, (HANK, HANK), 1)
    eye = row_id == col_id
    s_col = s_row.T
    recip = jnp.where(eye, 0.0, 1.0 / jnp.where(eye, 1.0, s_row * s_row - s_col * s_col))
    f_row[...] = recip * s_row
    f_col[...] = recip * s_col
    second_bar = product(accs, split(product(accs, u_ref, split(zbar))), wt_ref)
    for m, value in enumerate(diagonal_sums(second_bar)):
        second[m] = value

    arrived(recv_b, Z - 1, 1)
    recv_c[mine, :] = jnp.sum(recv_b[...].reshape(Z, PIECE, 128), axis=0)
    send(plane, lambda peer: recv_c.at[mine], recv_c.at[mine], 2)

    turn(4, 8)

    arrived(recv_c, GROUP - 1, 2)
    lane = lax.broadcasted_iota(jnp.int32, (L, 2 * L), 1)
    low = lane < L
    even = [recv_c[L * q : L * (q + 1), :] for q in range(4)]
    turned = [pltpu.roll(value, L, 1) for value in even]
    pairs = []
    for q in range(3):
        pairs.append(even[q])
        pairs.append(jnp.where(low, turned[q], turned[q + 1]))
    hankel = jnp.concatenate(
        [jnp.concatenate([pairs[i], pairs[i + 2]], axis=1) for i in range(K)], axis=0
    )
    quot = product(accs, ut_ref, split(hankel))
    zmat = product(accs, split(quot), w_ref)
    parts = split(zmat)
    left_term = product(accs, parts, zt_ref)
    right_term = product(accs, zt_ref, parts)
    sing_row = singv[...]
    sbar = -jnp.sum(factors[2] * zmat, axis=0, keepdims=True) / (sing_row * sing_row)
    core_mat = (
        f_row[...] * (left_term - left_term.T)
        - f_col[...] * (right_term - right_term.T)
        + jnp.where(eye, jnp.broadcast_to(sbar, (HANK, HANK)), 0.0)
    )
    first_bar = product(accs, split(product(accs, u_ref, split(core_mat))), wt_ref)

    sums = diagonal_sums(first_bar)
    sums = [sums[0]] + [sums[m] + second[m - 1] for m in range(1, 6)] + [second[5]]
    weights = [jnp.zeros((L, 2 * L), jnp.float32) for p in range(2)]
    zero = jnp.zeros((L, 2 * L), jnp.float32)
    for k in range(2 * K):
        here_k = sums[k] if k < 7 else zero
        before = sums[k - 1] if k > 0 else zero
        mixed = jnp.where(low, here_k, before)
        both = mixed + pltpu.roll(mixed, L, 1)
        for p in range(2):
            weights[p] = weights[p] + both * tabv[p, 8 + k : 9 + k, :]
    for p in range(2):
        w_out[:, 128 * p : 128 * (p + 1)] = weights[p].astype(jnp.bfloat16)

    sent = solv.at[0, pl.ds(0, 2 * PIECE * (2 * len(plane) + len(line)))]
    pltpu.make_async_copy(sent, sent, send_sem.at[0]).wait()


def reduce_kernel(*refs):
    quarters = [pltpu.ACC(unit)((HANK // 4, HANK), jnp.float32) for unit in (0, 0, 1, 1)]
    pl.run_scoped(functools.partial(reduce_body, *refs), *quarters)


def output_kernel(turned, w_ref, out, held, sem):
    half = turned.shape[0]
    size = OUT_ROWS
    zero = jnp.zeros((L, 256), jnp.bfloat16)
    wide = [jnp.concatenate([w_ref[...], zero], axis=0), jnp.concatenate([zero, w_ref[...]], axis=0)]
    for c in range(half // size):
        block = turned[c * size : (c + 1) * size, :]
        for h in range(2):
            res = dot(block, wide[h]).astype(jnp.bfloat16)
            part = pl.ds(h * half + c * size, size)
            for p in range(2):
                held[p, part, :] = res[:, 128 * p : 128 * (p + 1)]
            pltpu.make_async_copy(held.at[:, part], out.at[:, part], sem.at[0]).start()
    pltpu.make_async_copy(held, out, sem.at[0]).wait()


def per_device(solutions, probe, left_factor, singular, right_factor, reduced_adjoint):
    table = jnp.asarray(coefficient_table())
    depth = solutions.shape[1]
    hbm = pl.BlockSpec(memory_space=pltpu.HBM)
    vmem = pl.BlockSpec(memory_space=pltpu.VMEM)
    f32 = lambda *shape: pltpu.VMEM(shape, jnp.float32)
    bf16 = lambda *shape: pltpu.VMEM(shape, jnp.bfloat16)
    weights, turned = pl.pallas_call(
        reduce_kernel,
        name="moments",
        out_shape=[
            jax.ShapeDtypeStruct((L, 256), jnp.bfloat16),
            jax.ShapeDtypeStruct((depth // 2, 128), jnp.bfloat16),
        ],
        in_specs=[hbm] * 7,
        out_specs=[vmem] * 2,
        scratch_shapes=[
            bf16(2, depth, 128), bf16(L, depth), f32(3, HANK, HANK), f32(1, HANK), f32(2, 16, 128),
            f32(GROUP * PIECE, 128), f32(GROUP * PIECE, 128), f32(Z * PIECE, 128), f32(GROUP * PIECE, 128),
            *[bf16(2, HANK, HANK)] * 5, f32(HANK, HANK), f32(HANK, HANK), f32(6, L, 2 * L),
            pltpu.SemaphoreType.DMA((CHUNKS + 2,)), pltpu.SemaphoreType.DMA((3,)),
            pltpu.SemaphoreType.DMA((1,)), pltpu.SemaphoreType.DMA((3,)),
        ],
        compiler_params=pltpu.CompilerParams(
            collective_id=0, has_side_effects=True, vmem_limit_bytes=24 << 20
        ),
    )(
        *(
            pltpu.with_memory_space_constraint(array, pltpu.HBM)
            for array in (
                solutions, probe, left_factor, singular.reshape(1, HANK), right_factor, reduced_adjoint, table
            )
        )
    )
    return pl.pallas_call(
        output_kernel,
        name="output",
        out_shape=jax.ShapeDtypeStruct((2, depth, 128), jnp.bfloat16),
        in_specs=[vmem] * 2,
        out_specs=pl.BlockSpec(memory_space=pltpu.HBM),
        scratch_shapes=[bf16(2, depth, 128), pltpu.SemaphoreType.DMA((1,))],
        compiler_params=pltpu.CompilerParams(vmem_limit_bytes=24 << 20),
    )(turned, weights)


def solution(mesh):
    in_specs = (P("pts", "rows", None), P(None, "rows"), P(), P(), P(), P())
    out_specs = P("pts", "rows", None)
    return jax.shard_map(
        per_device, mesh=mesh, in_specs=in_specs, out_specs=out_specs, check_vma=False
    )
```

time: 30.4 us -> 29.3 us (0.964)
  Pallas kernels: 30.3 us -> 29.2 us
    pallas_call x1, Pallas kernels: 27.8 us -> 27 us  [per_device(): pl.pallas_call(reduce_kernel, name='moments', out_shape=[jax.ShapeDtypeSt...]
    pallas_call x1, Pallas kernels: 2.54 us -> 2.14 us  [per_device(): pl.pallas_call(output_kernel, name='output', out_shape=jax.ShapeDtypeStru...]
where the time goes in v3:
time: 29.3 us; the launch traced here: 29.2 us
  Pallas kernels  29.2 us (100%)
    pallas_call x1, Pallas kernels, per_device(): pl.pallas_call(reduce_kernel, name='moments', out_shape=[jax.ShapeDtypeSt...  27 us
    pallas_call x1, Pallas kernels, per_device(): pl.pallas_call(output_kernel, name='output', out_shape=jax.ShapeDtypeStru...  2.14 us

profile of v3, /device:TPU:1, one launch (start us, length us, event | category | flops | bytes accessed | tf_op | source)
XLA Modules:
  0.0 29.2 jit_solution(14001892976954383428)
XLA Ops:
  0.0 27.0 %moments.1 = (bf16[64,256]{1,0:T(8,128)(2,1)S(1)}, bf16[4096,128]{1,0:T(8,128)(2,1)S(1)}) custom-call(bf16[2,8192,128]{2,1,0:T(8,128)(2,1)} %refs_0_.1, bf16[64,8192]{1,0:T(8,128)(2,1)} %refs_1_.1, f32[256,256]{1,0:T(8,128)} %refs_2_.1, f32[1,256]{1,0:T(1,128)} %bitcast.1, f32[256,256]{1,0:T(8,128)} %refs_4_.1, f32[256,256]{1,0:T(8,128)} %refs_5_.1, ...), custom_call_target="tpu_custom_call" | custom-call | tf_op jit(solution)/shard_map/moments/pallas_call | solution.py:292
  27.0 2.1 %output.1 = bf16[2,8192,128]{2,1,0:T(8,128)(2,1)} custom-call(bf16[4096,128]{1,0:T(8,128)(2,1)S(1)} %get-tuple-element.7.turned, bf16[64,256]{1,0:T(8,128)(2,1)S(1)} %get-tuple-element.8.w_ref), custom_call_target="tpu_custom_call" | custom-call | tf_op jit(solution)/shard_map/output/pallas_call | solution.py:319

commit v4 on v3

--- a/solution.py
+++ b/solution.py
@@ -15,7 +15,8 @@
 PTS = 16
 MESH = pl.DeviceIdType.MESH
 X, Y, Z, CORES = 4, 4, 8, 2
-PIECE = 8
+OWNERS = 16
+PIECE = 16
 GROUP = X * Y * CORES
 CHUNKS = 8
 OUT_ROWS = 128
@@ -106,24 +107,31 @@
     tab = pltpu.make_async_copy(table.at[pl.ds(pts * 2, 2)], tabv, small_sem.at[0])
     tab.start()
 
-    xs = [lax.rem(x + d, X) * CORES for d in range(X)]
-    cores = [core, 1 - core]
-    ys = [lax.rem(y + d, Y) for d in range(Y)]
-    zs = [lax.rem(z + d, Z) * Y + y for d in range(Z)]
-    plane = []
-    for dx, dy in sorted(
-        [(i, j) for i in range(X) for j in range(Y)],
-        key=lambda d: -(min(d[0], X - d[0]) + min(d[1], Y - d[1])),
-    ):
-        for dc in range(CORES):
-            if dx or dy or dc:
-                other = xs[dx] + cores[dc]
-                plane.append((other, z * Y + ys[dy], ys[dy] * (X * CORES) + other))
-    line = [(pts, zs[d]) for d in sorted(range(1, Z), key=lambda d: -min(d, Z - d))]
+    owner = y < 2
+    spots = sorted(
+        [(p, j) for p in range(X * CORES) for j in range(Y)],
+        key=lambda d: (min(d[0] // CORES, X - d[0] // CORES) + min(d[1], Y - d[1]), -(d[0] % CORES)),
+    )
+    plane = [(p, z * Y + j, j * (X * CORES) + p) for p, j in spots]
+    owners = [peer + (j * X * CORES + p,) for peer, (p, j) in zip(plane, spots) if j < 2]
+    line = [(pts, lax.rem(z + d, Z) * Y + y, -1) for d in sorted(range(1, Z), key=lambda d: -min(d, Z - d))]
+    index = me
+
+    def each(peers, action):
+        for peer in peers:
+            pl.when(me != peer[2])(functools.partial(action, peer))
 
     barrier = pltpu.get_barrier_semaphore()
-    for p, r in line[:1] + [(p, r) for p, r, _ in plane] + line[1:]:
-        pl.semaphore_signal(barrier, inc=1, device_id=(p, r), device_id_type=MESH)
+
+    def announce(peer):
+        pl.semaphore_signal(barrier, inc=1, device_id=peer[:2], device_id_type=MESH)
+
+    @pl.when(owner)
+    def _():
+        each(plane[::-1], announce)
+        for peer in line:
+            announce(peer)
+
     small = [pltpu.make_async_copy(sing, singv, small_sem.at[1])]
     small += [pltpu.make_async_copy(ref, factors.at[i], small_sem.at[2]) for i, ref in enumerate((left, right, adj))]
     for copy in small:
@@ -154,26 +162,31 @@
     def piece(index):
         return pl.ds(pl.multiple_of(index * PIECE, PIECE), PIECE)
 
-    def send(peers, source, target, phase):
-        @pl.when(rows >= 0)
-        def _():
-            for peer in peers:
-                pltpu.make_async_remote_copy(
-                    src_ref=source(peer),
-                    dst_ref=target,
-                    send_sem=send_sem.at[0],
-                    recv_sem=recv_sem.at[phase],
-                    device_id=peer[:2],
-                    device_id_type=MESH,
-                ).start()
+    def send(source, target, phase, peer):
+        pltpu.make_async_remote_copy(
+            src_ref=source(peer),
+            dst_ref=target,
+            send_sem=send_sem.at[0],
+            recv_sem=recv_sem.at[phase],
+            device_id=peer[:2],
+            device_id_type=MESH,
+        ).start()
 
     def arrived(ref, count, phase):
         ref = ref.at[pl.ds(0, count * PIECE)]
         pltpu.make_async_copy(ref, ref, recv_sem.at[phase]).wait()
 
-    mine, here = piece(me), piece(z)
-    pl.semaphore_wait(barrier, len(plane) + len(line))
-    send(plane, lambda peer: send_a.at[piece(peer[2])], recv_a.at[mine], 0)
+    mine, here = piece(index), piece(z)
+
+    @pl.when(owner)
+    def _():
+        pl.semaphore_wait(barrier, OWNERS - 1 + Z - 1)
+
+    @pl.when(jnp.logical_not(owner))
+    def _():
+        pl.semaphore_wait(barrier, OWNERS)
+
+    each(owners, functools.partial(send, lambda peer: send_a.at[piece(peer[3])], recv_a.at[piece(me)], 0))
 
     def keep(ref, value):
         ref[0], ref[1] = split(value)
@@ -184,7 +197,10 @@
             pair = [probev[:, h * half + t * step : h * half + (t + 1) * step] for h in range(2)]
             turned_out[t * step : (t + 1) * step, :] = jnp.concatenate(pair, axis=0).T
 
-    recv_a[mine, :] = send_a[mine, :]
+    @pl.when(owner)
+    def _():
+        recv_a[piece(me), :] = send_a[mine, :]
+
     small[0].wait()
     pltpu.make_async_copy(factors, factors, small_sem.at[2]).wait()
     s_row = jnp.broadcast_to(singv[...], (HANK, HANK))
@@ -196,9 +212,12 @@
     keep(zt_ref, zbar.T)
     turn(0, 4)
 
-    arrived(recv_a, GROUP - 1, 0)
-    recv_b[here, :] = jnp.sum(recv_a[...].reshape(GROUP, PIECE, 128), axis=0)
-    send(line, lambda peer: recv_b.at[here], recv_b.at[here], 1)
+    @pl.when(owner)
+    def _():
+        arrived(recv_a, GROUP - 1, 0)
+        recv_b[here, :] = jnp.sum(recv_a[...].reshape(GROUP, PIECE, 128), axis=0)
+        for peer in line:
+            send(lambda peer: recv_b.at[here], recv_b.at[here], 1, peer)
 
     row_id = lax.broadcasted_iota(jnp.int32, (HANK, HANK), 0)
     col_id = lax.broadcasted_iota(jnp.int32, (HANK, HANK), 1)
@@ -211,13 +230,22 @@
     for m, value in enumerate(diagonal_sums(second_bar)):
         second[m] = value
 
-    arrived(recv_b, Z - 1, 1)
-    recv_c[mine, :] = jnp.sum(recv_b[...].reshape(Z, PIECE, 128), axis=0)
-    send(plane, lambda peer: recv_c.at[mine], recv_c.at[mine], 2)
+    @pl.when(owner)
+    def _():
+        arrived(recv_b, Z - 1, 1)
+        recv_c[mine, :] = jnp.sum(recv_b[...].reshape(Z, PIECE, 128), axis=0)
+        each(plane, functools.partial(send, lambda peer: recv_c.at[mine], recv_c.at[mine], 2))
 
     turn(4, 8)
 
-    arrived(recv_c, GROUP - 1, 2)
+    @pl.when(owner)
+    def _():
+        arrived(recv_c, OWNERS - 1, 2)
+
+    @pl.when(jnp.logical_not(owner))
+    def _():
+        arrived(recv_c, OWNERS, 2)
+
     lane = lax.broadcasted_iota(jnp.int32, (L, 2 * L), 1)
     low = lane < L
     even = [recv_c[L * q : L * (q + 1), :] for q in range(4)]
@@ -257,8 +285,17 @@
     for p in range(2):
         w_out[:, 128 * p : 128 * (p + 1)] = weights[p].astype(jnp.bfloat16)
 
-    sent = solv.at[0, pl.ds(0, 2 * PIECE * (2 * len(plane) + len(line)))]
-    pltpu.make_async_copy(sent, sent, send_sem.at[0]).wait()
+    def all_sent(count):
+        sent = solv.at[0, pl.ds(0, 2 * PIECE * count)]
+        pltpu.make_async_copy(sent, sent, send_sem.at[0]).wait()
+
+    @pl.when(owner)
+    def _():
+        all_sent(OWNERS - 1 + Z - 1 + GROUP - 1)
+
+    @pl.when(jnp.logical_not(owner))
+    def _():
+        all_sent(OWNERS)
 
 
 def reduce_kernel(*refs):
@@ -300,7 +337,7 @@
         out_specs=[vmem] * 2,
         scratch_shapes=[
             bf16(2, depth, 128), bf16(L, depth), f32(3, HANK, HANK), f32(1, HANK), f32(2, 16, 128),
-            f32(GROUP * PIECE, 128), f32(GROUP * PIECE, 128), f32(Z * PIECE, 128), f32(GROUP * PIECE, 128),
+            f32(OWNERS * PIECE, 128), f32(GROUP * PIECE, 128), f32(Z * PIECE, 128), f32(OWNERS * PIECE, 128),
             *[bf16(2, HANK, HANK)] * 5, f32(HANK, HANK), f32(HANK, HANK), f32(6, L, 2 * L),
             pltpu.SemaphoreType.DMA((CHUNKS + 2,)), pltpu.SemaphoreType.DMA((3,)),
             pltpu.SemaphoreType.DMA((1,)), pltpu.SemaphoreType.DMA((3,)),

time: 29.3 us -> 28.2 us (0.962)
  Pallas kernels: 29.2 us -> 28.1 us
    pallas_call x1, Pallas kernels: 27 us -> 25.9 us  [per_device(): pl.pallas_call(reduce_kernel, name='moments', out_shape=[jax.ShapeDtypeSt...]
where the time goes in v4:
time: 28.2 us; the launch traced here: 28.1 us
  Pallas kernels  28.1 us (100%)
    pallas_call x1, Pallas kernels, per_device(): pl.pallas_call(reduce_kernel, name='moments', out_shape=[jax.ShapeDtypeSt...  25.9 us
    pallas_call x1, Pallas kernels, per_device(): pl.pallas_call(output_kernel, name='output', out_shape=jax.ShapeDtypeStru...  2.14 us

profile of v4, /device:TPU:1, one launch (start us, length us, event | category | flops | bytes accessed | tf_op | source)
XLA Modules:
  0.0 28.1 jit_solution(12571892526936567666)
XLA Ops:
  0.0 25.9 %moments.1 = (bf16[64,256]{1,0:T(8,128)(2,1)S(1)}, bf16[4096,128]{1,0:T(8,128)(2,1)S(1)}) custom-call(bf16[2,8192,128]{2,1,0:T(8,128)(2,1)} %refs_0_.1, bf16[64,8192]{1,0:T(8,128)(2,1)} %refs_1_.1, f32[256,256]{1,0:T(8,128)} %refs_2_.1, f32[1,256]{1,0:T(1,128)} %bitcast.1, f32[256,256]{1,0:T(8,128)} %refs_4_.1, f32[256,256]{1,0:T(8,128)} %refs_5_.1, ...), custom_call_target="tpu_custom_call" | custom-call | tf_op jit(solution)/shard_map/moments/pallas_call | solution.py:329
  26.0 2.1 %output.1 = bf16[2,8192,128]{2,1,0:T(8,128)(2,1)} custom-call(bf16[4096,128]{1,0:T(8,128)(2,1)S(1)} %get-tuple-element.7.turned, bf16[64,256]{1,0:T(8,128)(2,1)S(1)} %get-tuple-element.8.w_ref), custom_call_target="tpu_custom_call" | custom-call | tf_op jit(solution)/shard_map/output/pallas_call | solution.py:356

commit v5 on v4

--- a/solution.py
+++ b/solution.py
@@ -15,7 +15,7 @@
 PTS = 16
 MESH = pl.DeviceIdType.MESH
 X, Y, Z, CORES = 4, 4, 8, 2
-OWNERS = 16
+OWNERS = 14
 PIECE = 16
 GROUP = X * Y * CORES
 CHUNKS = 8
@@ -107,15 +107,19 @@
     tab = pltpu.make_async_copy(table.at[pl.ds(pts * 2, 2)], tabv, small_sem.at[0])
     tab.start()
 
-    owner = y < 2
+    owner = (y == 0) | ((y == 1) & (x != 2))
     spots = sorted(
         [(p, j) for p in range(X * CORES) for j in range(Y)],
         key=lambda d: (min(d[0] // CORES, X - d[0] // CORES) + min(d[1], Y - d[1]), -(d[0] % CORES)),
     )
     plane = [(p, z * Y + j, j * (X * CORES) + p) for p, j in spots]
-    owners = [peer + (j * X * CORES + p,) for peer, (p, j) in zip(plane, spots) if j < 2]
+    owners = [
+        peer + (j * (X * CORES - p // (3 * CORES) * CORES) + p,)
+        for peer, (p, j) in zip(plane, spots)
+        if j == 0 or (j == 1 and p // CORES != 2)
+    ]
     line = [(pts, lax.rem(z + d, Z) * Y + y, -1) for d in sorted(range(1, Z), key=lambda d: -min(d, Z - d))]
-    index = me
+    index = y * (X * CORES - lax.div(x, 3) * CORES) + pts
 
     def each(peers, action):
         for peer in peers:
@@ -157,7 +161,10 @@
             own = gram[:, 128 * p : 128 * (p + 1)]
             term = own * tabv[p, q : q + 1, :] + pltpu.roll(own, L, 1) * tabv[p, 4 + q : 5 + q, :]
             total = term if total is None else total + term
-        send_a[L * q : L * (q + 1), :] = total
+        if q < 3:
+            send_a[L * q : L * (q + 1), :] = total
+        else:
+            send_a[L * q :, :] = total[: L // 2] + pltpu.roll(total[L // 2 :], L, 1)
 
     def piece(index):
         return pl.ds(pl.multiple_of(index * PIECE, PIECE), PIECE)
@@ -186,7 +193,7 @@
     def _():
         pl.semaphore_wait(barrier, OWNERS)
 
-    each(owners, functools.partial(send, lambda peer: send_a.at[piece(peer[3])], recv_a.at[piece(me)], 0))
+    each(owners[::-1], functools.partial(send, lambda peer: send_a.at[piece(peer[3])], recv_a.at[piece(me)], 0))
 
     def keep(ref, value):
         ref[0], ref[1] = split(value)
@@ -248,8 +255,10 @@
 
     lane = lax.broadcasted_iota(jnp.int32, (L, 2 * L), 1)
     low = lane < L
-    even = [recv_c[L * q : L * (q + 1), :] for q in range(4)]
+    even = [recv_c[L * q : L * (q + 1), :] for q in range(3)]
+    last = recv_c[3 * L :, :]
     turned = [pltpu.roll(value, L, 1) for value in even]
+    turned.append(jnp.concatenate([pltpu.roll(last, L, 1), last], axis=0))
     pairs = []
     for q in range(3):
         pairs.append(even[q])

time: 28.2 us -> 27.9 us (0.989)
  Pallas kernels: 28.1 us -> 27.7 us
    pallas_call x1, Pallas kernels: 25.9 us -> 25.5 us  [per_device(): pl.pallas_call(reduce_kernel, name='moments', out_shape=[jax.ShapeDtypeSt...]
where the time goes in v5:
time: 27.9 us; the launch traced here: 27.7 us
  Pallas kernels  27.7 us (99%)
    pallas_call x1, Pallas kernels, per_device(): pl.pallas_call(reduce_kernel, name='moments', out_shape=[jax.ShapeDtypeSt...  25.5 us
    pallas_call x1, Pallas kernels, per_device(): pl.pallas_call(output_kernel, name='output', out_shape=jax.ShapeDtypeStru...  2.14 us

profile of v5, /device:TPU:1, one launch (start us, length us, event | category | flops | bytes accessed | tf_op | source)
XLA Modules:
  0.0 27.7 jit_solution(17191416157354871286)
XLA Ops:
  0.0 25.5 %moments.1 = (bf16[64,256]{1,0:T(8,128)(2,1)S(1)}, bf16[4096,128]{1,0:T(8,128)(2,1)S(1)}) custom-call(bf16[2,8192,128]{2,1,0:T(8,128)(2,1)} %refs_0_.1, bf16[64,8192]{1,0:T(8,128)(2,1)} %refs_1_.1, f32[256,256]{1,0:T(8,128)} %refs_2_.1, f32[1,256]{1,0:T(1,128)} %bitcast.1, f32[256,256]{1,0:T(8,128)} %refs_4_.1, f32[256,256]{1,0:T(8,128)} %refs_5_.1, ...), custom_call_target="tpu_custom_call" | custom-call | tf_op jit(solution)/shard_map/moments/pallas_call | solution.py:338
  25.5 2.1 %output.1 = bf16[2,8192,128]{2,1,0:T(8,128)(2,1)} custom-call(bf16[4096,128]{1,0:T(8,128)(2,1)S(1)} %get-tuple-element.7.turned, bf16[64,256]{1,0:T(8,128)(2,1)S(1)} %get-tuple-element.8.w_ref), custom_call_target="tpu_custom_call" | custom-call | tf_op jit(solution)/shard_map/output/pallas_call | solution.py:365

commit v6 on v5

--- a/solution.py
+++ b/solution.py
@@ -63,7 +63,24 @@
         for b in range(2):
             part = slice((2 * unit + b) * quarter, (2 * unit + b + 1) * quarter)
             pltpu.matmul_acc_lhs(accs[2 * unit + b], first[0][part], 1 if b == 0 else None)
-    return jnp.concatenate([pltpu.matmul_pop(acc) for acc in accs], axis=0)
+    return jnp.concatenate([pltpu.matmul_pop(acc) for acc in accs[:4]], axis=0)
+
+
+def both_products(accs, first, second):
+    for unit, (_, right) in enumerate((first, second)):
+        pltpu.matmul_push_rhs(right[0], 0, unit)
+        pltpu.matmul_push_rhs(right[1], 1, unit)
+    half = HANK // 2
+    for b in range(2):
+        part = slice(b * half, (b + 1) * half)
+        for unit, (left, _) in enumerate((first, second)):
+            pltpu.matmul_acc_lhs(accs[2 * unit + b], left[0][part], 0 if b == 0 else None)
+            pltpu.matmul_acc_lhs(accs[2 * unit + b], left[1][part])
+    for b in range(2):
+        part = slice(b * half, (b + 1) * half)
+        for unit, (left, _) in enumerate((first, second)):
+            pltpu.matmul_acc_lhs(accs[2 * unit + b], left[0][part], 1 if b == 0 else None)
+    return [jnp.concatenate([pltpu.matmul_pop(accs[2 * u + b]) for b in range(2)], axis=0) for u in range(2)]
 
 
 def diagonal_sums(full):
@@ -129,6 +146,8 @@
 
     def announce(peer):
         pl.semaphore_signal(barrier, inc=1, device_id=peer[:2], device_id_type=MESH)
+
+    announce((x * CORES + 1 - core, rows))
 
     @pl.when(owner)
     def _():
@@ -187,11 +206,11 @@
 
     @pl.when(owner)
     def _():
-        pl.semaphore_wait(barrier, OWNERS - 1 + Z - 1)
+        pl.semaphore_wait(barrier, OWNERS + Z - 1)
 
     @pl.when(jnp.logical_not(owner))
     def _():
-        pl.semaphore_wait(barrier, OWNERS)
+        pl.semaphore_wait(barrier, OWNERS + 1)
 
     each(owners[::-1], functools.partial(send, lambda peer: send_a.at[piece(peer[3])], recv_a.at[piece(me)], 0))
 
@@ -269,8 +288,7 @@
     quot = product(accs, ut_ref, split(hankel))
     zmat = product(accs, split(quot), w_ref)
     parts = split(zmat)
-    left_term = product(accs, parts, zt_ref)
-    right_term = product(accs, zt_ref, parts)
+    left_term, right_term = both_products(accs[4:], (parts, zt_ref), (zt_ref, parts))
     sing_row = singv[...]
     sbar = -jnp.sum(factors[2] * zmat, axis=0, keepdims=True) / (sing_row * sing_row)
     core_mat = (
@@ -308,8 +326,10 @@
 
 
 def reduce_kernel(*refs):
-    quarters = [pltpu.ACC(unit)((HANK // 4, HANK), jnp.float32) for unit in (0, 0, 1, 1)]
-    pl.run_scoped(functools.partial(reduce_body, *refs), *quarters)
+    parts = [
+        pltpu.ACC(unit)((HANK // share, HANK), jnp.float32) for share in (4, 2) for unit in (0, 0, 1, 1)
+    ]
+    pl.run_scoped(functools.partial(reduce_body, *refs), *parts)
 
 
 def output_kernel(turned, w_ref, out, held, sem):

time: 27.9 us -> 27.9 us (level)
  no operation moved by 1% of the time
where the time goes in v6:
time: 27.9 us; the launch traced here: 27.7 us
  Pallas kernels  27.7 us (99%)
    pallas_call x1, Pallas kernels, per_device(): pl.pallas_call(reduce_kernel, name='moments', out_shape=[jax.ShapeDtypeSt...  25.6 us
    pallas_call x1, Pallas kernels, per_device(): pl.pallas_call(output_kernel, name='output', out_shape=jax.ShapeDtypeStru...  2.14 us

profile of v6, /device:TPU:1, one launch (start us, length us, event | category | flops | bytes accessed | tf_op | source)
XLA Modules:
  0.0 27.7 jit_solution(9297480619125729787)
XLA Ops:
  0.0 25.6 %moments.1 = (bf16[64,256]{1,0:T(8,128)(2,1)S(1)}, bf16[4096,128]{1,0:T(8,128)(2,1)S(1)}) custom-call(bf16[2,8192,128]{2,1,0:T(8,128)(2,1)} %refs_0_.1, bf16[64,8192]{1,0:T(8,128)(2,1)} %refs_1_.1, f32[256,256]{1,0:T(8,128)} %refs_2_.1, f32[1,256]{1,0:T(1,128)} %bitcast.1, f32[256,256]{1,0:T(8,128)} %refs_4_.1, f32[256,256]{1,0:T(8,128)} %refs_5_.1, ...), custom_call_target="tpu_custom_call" | custom-call | tf_op jit(solution)/shard_map/moments/pallas_call | solution.py:358
  25.6 2.1 %output.1 = bf16[2,8192,128]{2,1,0:T(8,128)(2,1)} custom-call(bf16[4096,128]{1,0:T(8,128)(2,1)S(1)} %get-tuple-element.7.turned, bf16[64,256]{1,0:T(8,128)(2,1)S(1)} %get-tuple-element.8.w_ref), custom_call_target="tpu_custom_call" | custom-call | tf_op jit(solution)/shard_map/output/pallas_call | solution.py:385

commit v7 on v6

--- a/solution.py
+++ b/solution.py
@@ -136,7 +136,7 @@
         if j == 0 or (j == 1 and p // CORES != 2)
     ]
     line = [(pts, lax.rem(z + d, Z) * Y + y, -1) for d in sorted(range(1, Z), key=lambda d: -min(d, Z - d))]
-    index = y * (X * CORES - lax.div(x, 3) * CORES) + pts
+    index = lax.rem(y * (X * CORES - lax.div(x, 3) * CORES) + pts, OWNERS)
 
     def each(peers, action):
         for peer in peers:

time: 27.9 us -> 27.9 us (level)
  no operation moved by 1% of the time
where the time goes in v7:
time: 27.9 us; the launch traced here: 27.7 us
  Pallas kernels  27.7 us (99%)
    pallas_call x1, Pallas kernels, per_device(): pl.pallas_call(reduce_kernel, name='moments', out_shape=[jax.ShapeDtypeSt...  25.5 us
    pallas_call x1, Pallas kernels, per_device(): pl.pallas_call(output_kernel, name='output', out_shape=jax.ShapeDtypeStru...  2.14 us

profile of v7, /device:TPU:1, one launch (start us, length us, event | category | flops | bytes accessed | tf_op | source)
XLA Modules:
  0.0 27.7 jit_solution(5519741095065066902)
XLA Ops:
  0.0 25.5 %moments.1 = (bf16[64,256]{1,0:T(8,128)(2,1)S(1)}, bf16[4096,128]{1,0:T(8,128)(2,1)S(1)}) custom-call(bf16[2,8192,128]{2,1,0:T(8,128)(2,1)} %refs_0_.1, bf16[64,8192]{1,0:T(8,128)(2,1)} %refs_1_.1, f32[256,256]{1,0:T(8,128)} %refs_2_.1, f32[1,256]{1,0:T(1,128)} %bitcast.1, f32[256,256]{1,0:T(8,128)} %refs_4_.1, f32[256,256]{1,0:T(8,128)} %refs_5_.1, ...), custom_call_target="tpu_custom_call" | custom-call | tf_op jit(solution)/shard_map/moments/pallas_call | solution.py:358
  25.6 2.1 %output.1 = bf16[2,8192,128]{2,1,0:T(8,128)(2,1)} custom-call(bf16[4096,128]{1,0:T(8,128)(2,1)S(1)} %get-tuple-element.7.turned, bf16[64,256]{1,0:T(8,128)(2,1)S(1)} %get-tuple-element.8.w_ref), custom_call_target="tpu_custom_call" | custom-call | tf_op jit(solution)/shard_map/output/pallas_call | solution.py:385
